TPU v7x, 32 devices: a whole 2x2x4 slice. The times are simulated.
32 devices in a mesh: tm: 4 (over y, x), rows: 2 (over core), cols: 4 (over z).
Axes of the slice: x: 2, y: 2, z: 4, core: 2. Of those that a mesh axis runs over, the one named last changes fastest.
Arguments:
- inputs: bfloat16 [4, 34, 32, 128], P('tm', 'rows', 'cols'), may hold values from -6 to 6
- cotangent: bfloat16 [4, 34, 32, 128], P('tm', 'rows', 'cols'), may hold values from -6 to 6
- weight_one: bfloat16 [27, 128, 128], replicated, may hold values from -0.109375 to 0.109375
- weight_two: bfloat16 [27, 128, 128], replicated, may hold values from -0.109375 to 0.109375
Outputs:
- grad_inputs: float32 [4, 34, 32, 128], P('tm', 'rows', 'cols')
- grad_one: float32 [27, 128, 128], P(None, ('tm', 'rows'), 'cols')
- grad_two: float32 [27, 128, 128], P(None, ('tm', 'rows'), 'cols')
All inputs are finite; a program needn't handle non-finite values.
Results may differ from a plain program's by a relative error of at most 0.0029.
Values may be sent and summed in bfloat16 or wider, within the bound.
A program may use at most 64 MiB of HBM per device.

v0:
```python
import jax
import jax.numpy as jnp
from jax import lax
from jax.sharding import PartitionSpec as P


def padded_2(cells, sides, width):
    for axis, dim in sides:
        count = lax.axis_size(axis)
        ends = count - 1
        head = lax.slice_in_dim(cells, 0, width, axis=dim)
        tail = lax.slice_in_dim(cells, cells.shape[dim] - width, cells.shape[dim], axis=dim)
        cells = jnp.concatenate(
            [
                lax.ppermute(tail, axis, [(i, (i + 1) % count) for i in range(ends)]),
                cells,
                lax.ppermute(head, axis, [((i + 1) % count, i) for i in range(ends)]),
            ],
            axis=dim,
        )
    return cells


def from_behind(value, axis, steps):
    count = lax.axis_size(axis)
    leading, last = (max(0, -steps), min(count, count - steps))
    return lax.ppermute(value, axis, [(source, source + steps) for source in range(leading, last)])


def faces(source):
    return padded_2(source, (("rows", 1), ("cols", 2)), 1)


def earlier(source):
    frames = []
    for distance in (2, 1):
        frames.append(from_behind(source, "tm", distance))
    return jnp.concatenate(frames + [source], axis=0)


def later(source):
    frames = [source]
    for distance in (1, 2):
        frames.append(from_behind(source, "tm", -distance))
    return jnp.concatenate(frames, axis=0)


def past_taps(padded, rows_here, cols_here):
    pieces = []
    for t_off in range(3):
        for h_off in range(3):
            for w_off in range(3):
                pieces.append(padded[t_off, h_off : h_off + rows_here, w_off : w_off + cols_here])
    return jnp.concatenate(pieces, axis=-1).reshape(rows_here * cols_here, -1)


def future_taps(padded, rows_here, cols_here):
    pieces = []
    for t_off in range(3):
        for h_off in range(3):
            for w_off in range(3):
                pieces.append(
                    padded[
                        2 - t_off,
                        2 - h_off : 2 - h_off + rows_here,
                        2 - w_off : 2 - w_off + cols_here,
                    ]
                )
    return jnp.concatenate(pieces, axis=-1).reshape(rows_here * cols_here, -1)


def multiply(left, right):
    return jnp.dot(left, right, preferred_element_type=jnp.float32)


def contract_cells(taps, right):
    return lax.dot_general(
        taps, right, (((0,), (0,)), ((), ())), preferred_element_type=jnp.float32
    )


def body(inputs, cotangent, weight_one, weight_two):
    rows_here = inputs.shape[1]
    cols_here = inputs.shape[2]
    channels = inputs.shape[3]
    forward_one = weight_one.reshape(27 * channels, channels)
    adjoint_one = jnp.swapaxes(weight_one, 1, 2).reshape(27 * channels, channels)
    adjoint_two = jnp.swapaxes(weight_two, 1, 2).reshape(27 * channels, channels)
    both_faces = faces(jnp.concatenate([inputs, cotangent], axis=0))
    input_block = earlier(both_faces[0:1])
    grad_block = later(both_faces[1:2])
    input_taps = past_taps(input_block, rows_here, cols_here)
    hidden = multiply(input_taps, forward_one)
    squash = jax.nn.sigmoid(hidden)
    activation = (hidden * squash).astype(jnp.bfloat16)
    grad_act = multiply(future_taps(grad_block, rows_here, cols_here), adjoint_two)
    grad_hidden = (grad_act * squash * (1.0 + hidden * (1.0 - squash))).astype(jnp.bfloat16)
    act_block = earlier(faces(activation.reshape(1, rows_here, cols_here, channels)))
    flat_grad = cotangent.reshape(rows_here * cols_here, channels)
    partial_two = contract_cells(past_taps(act_block, rows_here, cols_here), flat_grad).reshape(
        27, channels, channels
    )
    hidden_block = later(faces(grad_hidden.reshape(1, rows_here, cols_here, channels)))
    back = multiply(future_taps(hidden_block, rows_here, cols_here), adjoint_one)
    grad_inputs = cotangent.astype(jnp.float32) + back.reshape(1, rows_here, cols_here, channels)
    partial_one = contract_cells(input_taps, grad_hidden).reshape(27, channels, channels)
    first, second = (
        lax.psum_scatter(partial_one, "cols", scatter_dimension=2, tiled=True),
        lax.psum_scatter(partial_two, "cols", scatter_dimension=2, tiled=True),
    )
    grad_one, grad_two = (
        lax.psum_scatter(first, ("tm", "rows"), scatter_dimension=1, tiled=True),
        lax.psum_scatter(second, ("tm", "rows"), scatter_dimension=1, tiled=True),
    )
    return (grad_inputs, grad_one, grad_two)


def solution(mesh):
    placed = (P("tm", "rows", "cols", None), P("tm", "rows", "cols", None), P(), P())
    return jax.shard_map(
        body,
        mesh=mesh,
        in_specs=placed,
        out_specs=(
            P("tm", "rows", "cols", None),
            P(None, ("tm", "rows"), "cols"),
            P(None, ("tm", "rows"), "cols"),
        ),
        check_vma=False,
    )
```

profile of v0, /device:TPU:0, one launch (start us, length us, event | category | flops | bytes accessed | tf_op | source)
XLA Modules:
  0.0 221.3 jit_solution(11365136958594522526)
XLA Ops:
  8.8 2.4 %collective-permute-start = (bf16[2,1,8,128]{3,2,1,0:T(8,128)(2,1)S(1)}, bf16[2,1,8,128]{3,2,1,0:T(8,128)(2,1)S(1)}, u32[]{:S(2)}, u32[]{:S(2)}) collective-permute-start(bf16[2,1,8,128]{3,2,1,0:T(8,128)(2,1)S(1)} %get-tuple-element.28), channel_id=1, source_target_pairs={{0,4},{1,5},{2,6},{3,7},{8,12},{9,13},{10,14},{11,15},{16,20},{17,... | collective-permute-start | bytes 12296 | tf_op jit(solution)/shard_map/ppermute | solution.py:15
  11.2 1.3 collective-permute-start.1
  12.5 1.8 collective-permute-done.1
  14.3 4.3 %collective-permute-start.2 = (bf16[2,19,1,128]{3,2,1,0:T(2,128)(2,1)S(1)}, bf16[2,19,1,128]{3,2,1,0:T(2,128)(2,1)S(1)}, u32[]{:S(2)}, u32[]{:S(2)}) collective-permute-start(bf16[2,19,1,128]{3,2,1,0:T(2,128)(2,1)S(1)} %get-tuple-element.26), channel_id=1, source_target_pairs={{0,1},{1,2},{2,3},{4,5},{5,6},{6,7},{8,9},{9,10},{10,11},{12,13},{... | collective-permute-start | bytes 29192 | tf_op jit(solution)/shard_map/ppermute | solution.py:15
  18.6 1.3 collective-permute-start.3
  19.9 1.9 copy.16
  21.8 1.3 copy.17
  24.4 1.3 collective-permute-start.4
  25.7 1.3 collective-permute-start.5
  27.0 5.5 %collective-permute-start.6 = (bf16[1,19,10,128]{3,2,1,0:T(8,128)(2,1)S(1)}, bf16[1,19,10,128]{3,2,1,0:T(8,128)(2,1)S(1)}, u32[]{:S(2)}, u32[]{:S(2)}) collective-permute-start(bf16[1,19,10,128]{3,2,1,0:T(8,128)(2,1)S(1)} %get-tuple-element.22), channel_id=1, source_target_pairs={{0,16},{8,24},{1,17},{9,25},{2,18},{10,26},{3,19},{11,27},{4,20},{... | collective-permute-start | bytes 145928 | tf_op jit(solution)/shard_map/ppermute | solution.py:27
  32.5 3.6 %collective-permute-start.7 = (bf16[1,19,10,128]{3,2,1,0:T(8,128)(2,1)S(1)}, bf16[1,19,10,128]{3,2,1,0:T(8,128)(2,1)S(1)}, u32[]{:S(2)}, u32[]{:S(2)}) collective-permute-start(bf16[1,19,10,128]{3,2,1,0:T(8,128)(2,1)S(1)} %get-tuple-element.22), channel_id=1, source_target_pairs={{0,8},{8,16},{16,24},{1,9},{9,17},{17,25},{2,10},{10,18},{18,26},{... | collective-permute-start | bytes 145928 | tf_op jit(solution)/shard_map/ppermute | solution.py:27
  36.5 1.7 collective-permute-done.7
  41.0 1.3 collective-permute-start.15
  42.7 1.7 fusion.6
  44.5 3.0 %collective-permute-start.8 = (bf16[1,1,8,128]{3,2,1,0:T(8,128)(2,1)S(1)}, bf16[1,1,8,128]{3,2,1,0:T(8,128)(2,1)S(1)}, u32[]{:S(2)}, u32[]{:S(2)}) collective-permute-start(bf16[1,1,8,128]{3,2,1,0:T(8,128)(2,1)S(1)} %get-tuple-element.40), channel_id=1, source_target_pairs={{0,4},{1,5},{2,6},{3,7},{8,12},{9,13},{10,14},{11,15},{16,20},{17,... | collective-permute-start | bytes 6152 | tf_op jit(solution)/shard_map/ppermute | solution.py:15
  47.6 1.3 collective-permute-start.9
  48.9 3.5 %collective-permute-start.16 = (bf16[1,19,1,128]{3,2,1,0:T(2,128)(2,1)S(1)}, bf16[1,19,1,128]{3,2,1,0:T(2,128)(2,1)S(1)}, u32[]{:S(2)}, u32[]{:S(2)}) collective-permute-start(bf16[1,19,1,128]{3,2,1,0:T(2,128)(2,1)S(1)} %get-tuple-element.32), channel_id=1, source_target_pairs={{0,1},{1,2},{2,3},{4,5},{5,6},{6,7},{8,9},{9,10},{10,11},{12,13},{... | collective-permute-start | bytes 14600 | tf_op jit(solution)/shard_map/ppermute | solution.py:15
  52.4 1.3 collective-permute-start.17
  53.8 4.5 %collective-permute-start.10 = (bf16[1,19,1,128]{3,2,1,0:T(2,128)(2,1)S(1)}, bf16[1,19,1,128]{3,2,1,0:T(2,128)(2,1)S(1)}, u32[]{:S(2)}, u32[]{:S(2)}) collective-permute-start(bf16[1,19,1,128]{3,2,1,0:T(2,128)(2,1)S(1)} %get-tuple-element.36), channel_id=1, source_target_pairs={{0,1},{1,2},{2,3},{4,5},{5,6},{6,7},{8,9},{9,10},{10,11},{12,13},{... | collective-permute-start | bytes 14600 | tf_op jit(solution)/shard_map/ppermute | solution.py:15
  58.3 1.3 collective-permute-start.11
  59.7 3.7 %collective-permute-start.18 = (bf16[1,19,10,128]{3,2,1,0:T(8,128)(2,1)S(1)}, bf16[1,19,10,128]{3,2,1,0:T(8,128)(2,1)S(1)}, u32[]{:S(2)}, u32[]{:S(2)}) collective-permute-start(bf16[1,19,10,128]{3,2,1,0:T(8,128)(2,1)S(1)} %pad_maximum_fusion.4), channel_id=1, source_target_pairs={{0,16},{8,24},{1,17},{9,25},{2,18},{10,26},{3,19},{11,27},{4,20},{... | collective-permute-start | bytes 145928 | tf_op jit(solution)/shard_map/ppermute | solution.py:27
  63.4 1.8 collective-permute-start.19
  65.4 1.3 collective-permute-start.12
  68.8 1.7 fusion.3
  73.2 12.2 %reduce-scatter.5.cloned.1.call-done = f32[27,128,32]{1,2,0:T(8,128)} async-done(((f32[27,128,128]{1,2,0:T(8,128)}), f32[27,128,32]{1,2,0:T(8,128)}) %reduce-scatter.5.cloned.1.call-update) | async-done | bytes 442384 | tf_op jit(solution)/shard_map/reduce_scatter | solution.py:108
  85.4 3.9 %copy.19 = f32[27,128,32]{2,0,1:T(8,128)} copy(f32[27,128,32]{1,2,0:T(8,128)} %reduce-scatter.5.cloned.1.call-done) | data formatting | bytes 884736 | tf_op jit(solution)/shard_map/reduce_scatter | solution.py:108
  89.4 35.8 %reduce-scatter.9.cloned.1.call-done = f32[27,128,32]{1,2,0:T(8,128)} async-done(((f32[27,128,128]{1,2,0:T(8,128)}), f32[27,128,32]{1,2,0:T(8,128)}) %reduce-scatter.9.cloned.1.call-update) | async-done | bytes 442384 | tf_op jit(solution)/shard_map/reduce_scatter | solution.py:109
  125.3 3.8 %copy.21 = f32[27,128,32]{2,0,1:T(8,128)} copy(f32[27,128,32]{1,2,0:T(8,128)} %reduce-scatter.9.cloned.1.call-done) | data formatting | bytes 884736 | tf_op jit(solution)/shard_map/reduce_scatter | solution.py:109
  130.2 38.4 %reduce-scatter.7.cloned.1.call-done = f32[27,16,32]{2,0,1:T(8,128)} async-done(((f32[27,128,32]{2,0,1:T(8,128)}), f32[27,16,32]{2,0,1:T(8,128)}) %reduce-scatter.7.cloned.1.call-update) | async-done | bytes 55312 | tf_op jit(solution)/shard_map/reduce_scatter | solution.py:112
  168.7 1.8 copy.22
  170.4 42.5 %reduce-scatter.11.cloned.1.call-done = f32[27,16,32]{2,0,1:T(8,128)} async-done(((f32[27,128,32]{2,0,1:T(8,128)}), f32[27,16,32]{2,0,1:T(8,128)}) %reduce-scatter.11.cloned.1.call-update) | async-done | bytes 55312 | tf_op jit(solution)/shard_map/reduce_scatter | solution.py:113
  213.0 1.8 copy.23
  (156 shorter events, 12.4 us)
Async XLA Ops:
  7.2 14.7 %copy-start = (bf16[27,128,128]{2,1,0:T(8,128)(2,1)S(1)}, bf16[27,128,128]{2,1,0:T(8,128)(2,1)}, u32[]{:S(2)}) copy-start(bf16[27,128,128]{2,1,0:T(8,128)(2,1)} %param.6) | copy-start | bytes 2654212
  7.2 78.3 %reduce-scatter.5.cloned.1.call-start = ((), (), s32[]{:S(2)}) async-start(), calls=%async_computation.4 | async-start | bytes 2211840 | tf_op jit(solution)/shard_map/reduce_scatter | solution.py:108
  8.8 3.7 %collective-permute-start = (bf16[2,1,8,128]{3,2,1,0:T(8,128)(2,1)S(1)}, bf16[2,1,8,128]{3,2,1,0:T(8,128)(2,1)S(1)}, u32[]{:S(2)}, u32[]{:S(2)}) collective-permute-start(bf16[2,1,8,128]{3,2,1,0:T(8,128)(2,1)S(1)} %get-tuple-element.28), channel_id=1, source_target_pairs={{0,4},{1,5},{2,6},{3,7},{8,12},{9,13},{10,14},{11,15},{16,20},{17,... | collective-permute-start | bytes 12296 | tf_op jit(solution)/shard_map/ppermute | solution.py:15
  11.2 3.1 %collective-permute-start.1 = (bf16[2,1,8,128]{3,2,1,0:T(8,128)(2,1)S(1)}, bf16[2,1,8,128]{3,2,1,0:T(8,128)(2,1)S(1)}, u32[]{:S(2)}, u32[]{:S(2)}) collective-permute-start(bf16[2,1,8,128]{3,2,1,0:T(8,128)(2,1)S(1)} %get-tuple-element.29), channel_id=1, source_target_pairs={{4,0},{5,1},{6,2},{7,3},{12,8},{13,9},{14,10},{15,11},{20,16},{21,... | collective-permute-start | bytes 12296 | tf_op jit(solution)/shard_map/ppermute | solution.py:17
  14.3 8.8 %collective-permute-start.2 = (bf16[2,19,1,128]{3,2,1,0:T(2,128)(2,1)S(1)}, bf16[2,19,1,128]{3,2,1,0:T(2,128)(2,1)S(1)}, u32[]{:S(2)}, u32[]{:S(2)}) collective-permute-start(bf16[2,19,1,128]{3,2,1,0:T(2,128)(2,1)S(1)} %get-tuple-element.26), channel_id=1, source_target_pairs={{0,1},{1,2},{2,3},{4,5},{5,6},{6,7},{8,9},{9,10},{10,11},{12,13},{... | collective-permute-start | bytes 29192 | tf_op jit(solution)/shard_map/ppermute | solution.py:15
  18.6 5.7 %collective-permute-start.3 = (bf16[2,19,1,128]{3,2,1,0:T(2,128)(2,1)S(1)}, bf16[2,19,1,128]{3,2,1,0:T(2,128)(2,1)S(1)}, u32[]{:S(2)}, u32[]{:S(2)}) collective-permute-start(bf16[2,19,1,128]{3,2,1,0:T(2,128)(2,1)S(1)} %get-tuple-element.27), channel_id=1, source_target_pairs={{1,0},{2,1},{3,2},{5,4},{6,5},{7,6},{9,8},{10,9},{11,10},{13,12},{... | collective-permute-start | bytes 29192 | tf_op jit(solution)/shard_map/ppermute | solution.py:17
  24.4 14.6 %copy-start.2 = (bf16[1,17,8,128]{3,2,1,0:T(8,128)(2,1)S(1)}, bf16[1,17,8,128]{3,2,1,0:T(8,128)(2,1)}, u32[]{:S(2)}) copy-start(bf16[1,17,8,128]{3,2,1,0:T(8,128)(2,1)} %param.4) | copy-start | bytes 104452
  24.4 14.0 %collective-permute-start.4 = (bf16[1,19,10,128]{3,2,1,0:T(8,128)(2,1)S(1)}, bf16[1,19,10,128]{3,2,1,0:T(8,128)(2,1)S(1)}, u32[]{:S(2)}, u32[]{:S(2)}) collective-permute-start(bf16[1,19,10,128]{3,2,1,0:T(8,128)(2,1)S(1)} %get-tuple-element.23), channel_id=1, source_target_pairs={{16,0},{24,8},{17,1},{25,9},{18,2},{26,10},{19,3},{27,11},{20,4},{... | collective-permute-start | bytes 145928 | tf_op jit(solution)/shard_map/ppermute | solution.py:27
  25.7 12.9 %collective-permute-start.5 = (bf16[1,19,10,128]{3,2,1,0:T(8,128)(2,1)S(1)}, bf16[1,19,10,128]{3,2,1,0:T(8,128)(2,1)S(1)}, u32[]{:S(2)}, u32[]{:S(2)}) collective-permute-start(bf16[1,19,10,128]{3,2,1,0:T(8,128)(2,1)S(1)} %get-tuple-element.23), channel_id=1, source_target_pairs={{8,0},{16,8},{24,16},{9,1},{17,9},{25,17},{10,2},{18,10},{26,18},{... | collective-permute-start | bytes 145928 | tf_op jit(solution)/shard_map/ppermute | solution.py:27
  27.0 12.0 %copy-start.1 = (bf16[1,17,8,128]{3,2,1,0:T(8,128)(2,1)S(1)}, bf16[1,17,8,128]{3,2,1,0:T(8,128)(2,1)}, u32[]{:S(2)}) copy-start(bf16[1,17,8,128]{3,2,1,0:T(8,128)(2,1)} %param.5) | copy-start | bytes 104452
  27.0 9.2 %collective-permute-start.6 = (bf16[1,19,10,128]{3,2,1,0:T(8,128)(2,1)S(1)}, bf16[1,19,10,128]{3,2,1,0:T(8,128)(2,1)S(1)}, u32[]{:S(2)}, u32[]{:S(2)}) collective-permute-start(bf16[1,19,10,128]{3,2,1,0:T(8,128)(2,1)S(1)} %get-tuple-element.22), channel_id=1, source_target_pairs={{0,16},{8,24},{1,17},{9,25},{2,18},{10,26},{3,19},{11,27},{4,20},{... | collective-permute-start | bytes 145928 | tf_op jit(solution)/shard_map/ppermute | solution.py:27
  32.5 5.6 %collective-permute-start.7 = (bf16[1,19,10,128]{3,2,1,0:T(8,128)(2,1)S(1)}, bf16[1,19,10,128]{3,2,1,0:T(8,128)(2,1)S(1)}, u32[]{:S(2)}, u32[]{:S(2)}) collective-permute-start(bf16[1,19,10,128]{3,2,1,0:T(8,128)(2,1)S(1)} %get-tuple-element.22), channel_id=1, source_target_pairs={{0,8},{8,16},{16,24},{1,9},{9,17},{17,25},{2,10},{10,18},{18,26},{... | collective-permute-start | bytes 145928 | tf_op jit(solution)/shard_map/ppermute | solution.py:27
  39.7 9.2 %collective-permute-start.14 = (bf16[1,1,8,128]{3,2,1,0:T(8,128)(2,1)S(1)}, bf16[1,1,8,128]{3,2,1,0:T(8,128)(2,1)S(1)}, u32[]{:S(2)}, u32[]{:S(2)}) collective-permute-start(bf16[1,1,8,128]{3,2,1,0:T(8,128)(2,1)S(1)} %get-tuple-element.38), channel_id=1, source_target_pairs={{0,4},{1,5},{2,6},{3,7},{8,12},{9,13},{10,14},{11,15},{16,20},{17,... | collective-permute-start | bytes 6152 | tf_op jit(solution)/shard_map/ppermute | solution.py:15
  41.0 7.9 %collective-permute-start.15 = (bf16[1,1,8,128]{3,2,1,0:T(8,128)(2,1)S(1)}, bf16[1,1,8,128]{3,2,1,0:T(8,128)(2,1)S(1)}, u32[]{:S(2)}, u32[]{:S(2)}) collective-permute-start(bf16[1,1,8,128]{3,2,1,0:T(8,128)(2,1)S(1)} %get-tuple-element.39), channel_id=1, source_target_pairs={{4,0},{5,1},{6,2},{7,3},{12,8},{13,9},{14,10},{15,11},{20,16},{21,... | collective-permute-start | bytes 6152 | tf_op jit(solution)/shard_map/ppermute | solution.py:17
  44.5 80.8 %reduce-scatter.9.cloned.1.call-start = ((), (), s32[]{:S(2)}) async-start(), calls=%async_computation.6 | async-start | bytes 2211840 | tf_op jit(solution)/shard_map/reduce_scatter | solution.py:109
  44.5 9.2 %collective-permute-start.8 = (bf16[1,1,8,128]{3,2,1,0:T(8,128)(2,1)S(1)}, bf16[1,1,8,128]{3,2,1,0:T(8,128)(2,1)S(1)}, u32[]{:S(2)}, u32[]{:S(2)}) collective-permute-start(bf16[1,1,8,128]{3,2,1,0:T(8,128)(2,1)S(1)} %get-tuple-element.40), channel_id=1, source_target_pairs={{0,4},{1,5},{2,6},{3,7},{8,12},{9,13},{10,14},{11,15},{16,20},{17,... | collective-permute-start | bytes 6152 | tf_op jit(solution)/shard_map/ppermute | solution.py:15
  47.6 6.2 %collective-permute-start.9 = (bf16[1,1,8,128]{3,2,1,0:T(8,128)(2,1)S(1)}, bf16[1,1,8,128]{3,2,1,0:T(8,128)(2,1)S(1)}, u32[]{:S(2)}, u32[]{:S(2)}) collective-permute-start(bf16[1,1,8,128]{3,2,1,0:T(8,128)(2,1)S(1)} %get-tuple-element.41), channel_id=1, source_target_pairs={{4,0},{5,1},{6,2},{7,3},{12,8},{13,9},{14,10},{15,11},{20,16},{21,... | collective-permute-start | bytes 6152 | tf_op jit(solution)/shard_map/ppermute | solution.py:17
  48.9 10.7 %collective-permute-start.16 = (bf16[1,19,1,128]{3,2,1,0:T(2,128)(2,1)S(1)}, bf16[1,19,1,128]{3,2,1,0:T(2,128)(2,1)S(1)}, u32[]{:S(2)}, u32[]{:S(2)}) collective-permute-start(bf16[1,19,1,128]{3,2,1,0:T(2,128)(2,1)S(1)} %get-tuple-element.32), channel_id=1, source_target_pairs={{0,1},{1,2},{2,3},{4,5},{5,6},{6,7},{8,9},{9,10},{10,11},{12,13},{... | collective-permute-start | bytes 14600 | tf_op jit(solution)/shard_map/ppermute | solution.py:15
  52.4 7.2 %collective-permute-start.17 = (bf16[1,19,1,128]{3,2,1,0:T(2,128)(2,1)S(1)}, bf16[1,19,1,128]{3,2,1,0:T(2,128)(2,1)S(1)}, u32[]{:S(2)}, u32[]{:S(2)}) collective-permute-start(bf16[1,19,1,128]{3,2,1,0:T(2,128)(2,1)S(1)} %get-tuple-element.33), channel_id=1, source_target_pairs={{1,0},{2,1},{3,2},{5,4},{6,5},{7,6},{9,8},{10,9},{11,10},{13,12},{... | collective-permute-start | bytes 14600 | tf_op jit(solution)/shard_map/ppermute | solution.py:17
  53.8 11.5 %collective-permute-start.10 = (bf16[1,19,1,128]{3,2,1,0:T(2,128)(2,1)S(1)}, bf16[1,19,1,128]{3,2,1,0:T(2,128)(2,1)S(1)}, u32[]{:S(2)}, u32[]{:S(2)}) collective-permute-start(bf16[1,19,1,128]{3,2,1,0:T(2,128)(2,1)S(1)} %get-tuple-element.36), channel_id=1, source_target_pairs={{0,1},{1,2},{2,3},{4,5},{5,6},{6,7},{8,9},{9,10},{10,11},{12,13},{... | collective-permute-start | bytes 14600 | tf_op jit(solution)/shard_map/ppermute | solution.py:15
  58.3 7.0 %collective-permute-start.11 = (bf16[1,19,1,128]{3,2,1,0:T(2,128)(2,1)S(1)}, bf16[1,19,1,128]{3,2,1,0:T(2,128)(2,1)S(1)}, u32[]{:S(2)}, u32[]{:S(2)}) collective-permute-start(bf16[1,19,1,128]{3,2,1,0:T(2,128)(2,1)S(1)} %get-tuple-element.37), channel_id=1, source_target_pairs={{1,0},{2,1},{3,2},{5,4},{6,5},{7,6},{9,8},{10,9},{11,10},{13,12},{... | collective-permute-start | bytes 14600 | tf_op jit(solution)/shard_map/ppermute | solution.py:17
  59.7 8.4 %collective-permute-start.18 = (bf16[1,19,10,128]{3,2,1,0:T(8,128)(2,1)S(1)}, bf16[1,19,10,128]{3,2,1,0:T(8,128)(2,1)S(1)}, u32[]{:S(2)}, u32[]{:S(2)}) collective-permute-start(bf16[1,19,10,128]{3,2,1,0:T(8,128)(2,1)S(1)} %pad_maximum_fusion.4), channel_id=1, source_target_pairs={{0,16},{8,24},{1,17},{9,25},{2,18},{10,26},{3,19},{11,27},{4,20},{... | collective-permute-start | bytes 145928 | tf_op jit(solution)/shard_map/ppermute | solution.py:27
  63.4 4.9 %collective-permute-start.19 = (bf16[1,19,10,128]{3,2,1,0:T(8,128)(2,1)S(1)}, bf16[1,19,10,128]{3,2,1,0:T(8,128)(2,1)S(1)}, u32[]{:S(2)}, u32[]{:S(2)}) collective-permute-start(bf16[1,19,10,128]{3,2,1,0:T(8,128)(2,1)S(1)} %pad_maximum_fusion.4), channel_id=1, source_target_pairs={{0,8},{8,16},{16,24},{1,9},{9,17},{17,25},{2,10},{10,18},{18,26},{... | collective-permute-start | bytes 145928 | tf_op jit(solution)/shard_map/ppermute | solution.py:27
  65.4 6.3 %collective-permute-start.12 = (bf16[1,19,10,128]{3,2,1,0:T(8,128)(2,1)S(1)}, bf16[1,19,10,128]{3,2,1,0:T(8,128)(2,1)S(1)}, u32[]{:S(2)}, u32[]{:S(2)}) collective-permute-start(bf16[1,19,10,128]{3,2,1,0:T(8,128)(2,1)S(1)} %pad_maximum_fusion.2), channel_id=1, source_target_pairs={{16,0},{24,8},{17,1},{25,9},{18,2},{26,10},{19,3},{27,11},{20,4},{... | collective-permute-start | bytes 145928 | tf_op jit(solution)/shard_map/ppermute | solution.py:27
  66.7 6.3 %collective-permute-start.13 = (bf16[1,19,10,128]{3,2,1,0:T(8,128)(2,1)S(1)}, bf16[1,19,10,128]{3,2,1,0:T(8,128)(2,1)S(1)}, u32[]{:S(2)}, u32[]{:S(2)}) collective-permute-start(bf16[1,19,10,128]{3,2,1,0:T(8,128)(2,1)S(1)} %pad_maximum_fusion.2), channel_id=1, source_target_pairs={{8,0},{16,8},{24,16},{9,1},{17,9},{25,17},{10,2},{18,10},{26,18},{... | collective-permute-start | bytes 145928 | tf_op jit(solution)/shard_map/ppermute | solution.py:27
  70.5 98.2 %reduce-scatter.7.cloned.1.call-start = ((), (), s32[]{:S(2)}) async-start(), calls=%async_computation.5 | async-start | bytes 2359296 | tf_op jit(solution)/shard_map/reduce_scatter | solution.py:112
  89.3 123.6 %reduce-scatter.11.cloned.1.call-start = ((), (), s32[]{:S(2)}) async-start(), calls=%async_computation.7 | async-start | bytes 2359296 | tf_op jit(solution)/shard_map/reduce_scatter | solution.py:113
Sparse Core Ops, SparseCore 0:
  44.6 40.7 reduce-scatter.4
  87.8 37.4 reduce-scatter.8
  128.5 40.0 reduce-scatter.6
  171.8 41.1 reduce-scatter.10
where the time goes:
time: 222 us; the launch traced here: 221 us
  waiting for transfers between devices  136 us (61%)
  starting transfers between devices  46.8 us (21%)
  local copies, waits for them, and re-layouts  18.1 us (8%)
  between operations  14.6 us (7%)
  matrix products  5.34 us (2%)
    reduce_scatter x1, waiting for transfers between devices, body(): lax.psum_scatter(second, ('tm', 'rows'), scatter_dimension=1, tiled=True)  42.5 us
    reduce_scatter x1, waiting for transfers between devices, body(): lax.psum_scatter(first, ('tm', 'rows'), scatter_dimension=1, tiled=True)  38.4 us
    reduce_scatter x1, waiting for transfers between devices, body(): lax.psum_scatter(partial_two, 'cols', scatter_dimension=2, tiled=True)  35.8 us
    ppermute x8, starting transfers between devices, from_behind(): lax.ppermute(value, axis, [(source, source + steps) for source in range(l...  19.8 us
    ppermute x6, starting transfers between devices, padded_2(): lax.ppermute(tail, axis, [(i, (i + 1) % count) for i in range(ends)])  19 us
    reduce_scatter x1, waiting for transfers between devices, body(): lax.psum_scatter(partial_one, 'cols', scatter_dimension=2, tiled=True)  12.2 us
    unnamed x101, local copies, waits for them, and re-layouts  9.52 us
    ppermute x6, starting transfers between devices, padded_2(): lax.ppermute(head, axis, [((i + 1) % count, i) for i in range(ends)])  7.75 us
  transfers between devices with their start and end apart: 24, of which 9 were waited for; matrix products, arithmetic and copies ran while one was open for 9% of the time, Pallas kernels for 0%

commit v1 on v0

v1 whole, which is shorter than its diff:
```python
import functools

import jax
import jax.numpy as jnp
from jax import lax
from jax.experimental import pallas as pl
from jax.experimental.pallas import tpu as pltpu
from jax.sharding import PartitionSpec as P

MESH = pl.DeviceIdType.MESH
NT = (((1,), (1,)), ((), ()))


def kernel(
    dims,
    block_ref,
    edge_ref,
    w1_ref,
    w2_ref,
    back_ref,
    one_ref,
    two_ref,
    gat,
    left,
    right,
    sx,
    sg,
    sh,
    sa,
    imc,
    w1r,
    w2r,
    lt,
    pp,
    edges_out,
    edges_in,
    stage,
    landed,
    acc,
    own_sem,
    blk_send,
    blk_recv,
    low_send,
    low_recv,
    high_send,
    high_recv,
    gh_send,
    gh_recv,
    rs_send,
    rs_recv,
):
    tmn, rn, zn, rows, cols, chunk, chunk_pad, slots = dims
    plane = tmn * rn
    height = rn * rows
    pitch = (height + 2) * cols
    cells = rows * cols
    frame_cells = height * cols
    span = tmn * pitch
    ochunk = 128 // zn
    tm, row, col = lax.axis_index("tm"), lax.axis_index("rows"), lax.axis_index("cols")
    me = tm * rn + row

    def place(index, z):
        return (index // rn, lax.rem(index, rn), z)

    has_low, has_high = col > 0, col < zn - 1

    barrier = pltpu.get_barrier_semaphore()

    def greet(index, z):
        pl.semaphore_signal(barrier, inc=1, device_id=place(index, z), device_id_type=MESH)

    for d in range(1, plane):
        greet(lax.rem(me + d, plane), col)

    @pl.when(has_low)
    def _():
        for d in range(plane):
            greet(lax.rem(me + d, plane), col - 1)

    @pl.when(has_high)
    def _():
        for d in range(plane):
            greet(lax.rem(me + d, plane), col + 1)

    for z in range(zn):

        @pl.when((z > col + 1) | (z < col - 1))
        def _():
            greet(me, z)

    own = pltpu.make_async_copy(block_ref, gat.at[me], own_sem)
    own.start()

    for k in range(27):
        w1r[:, 128 * k : 128 * (k + 1)] = w1_ref[128 * k : 128 * (k + 1), :]
        w2r[:, 128 * k : 128 * (k + 1)] = w2_ref[128 * k : 128 * (k + 1), :]
    for buffer in (sx, sg, sh):
        buffer[...] = jnp.zeros(buffer.shape, buffer.dtype)
    sa[...] = jnp.zeros(sa.shape, sa.dtype)
    lt[...] = jnp.zeros(lt.shape, lt.dtype)
    pp[...] = jnp.zeros(pp.shape, pp.dtype)

    beside = jnp.minimum(col, 1) + jnp.minimum(zn - 1 - col, 1)
    pl.semaphore_wait(barrier, plane - 1 + plane * beside + zn - 1 - beside)

    def send_block(d):
        peer = lax.rem(me + d, plane)
        return pltpu.make_async_remote_copy(
            src_ref=block_ref,
            dst_ref=gat.at[me],
            send_sem=blk_send.at[d],
            recv_sem=blk_recv.at[me],
            device_id=place(peer, col),
            device_id_type=MESH,
        )

    def send_low(d):
        return pltpu.make_async_remote_copy(
            src_ref=edge_ref.at[0],
            dst_ref=right.at[me],
            send_sem=low_send.at[d],
            recv_sem=low_recv.at[me],
            device_id=place(lax.rem(me + d, plane), col - 1),
            device_id_type=MESH,
        )

    def send_high(d):
        return pltpu.make_async_remote_copy(
            src_ref=edge_ref.at[1],
            dst_ref=left.at[me],
            send_sem=high_send.at[d],
            recv_sem=high_recv.at[me],
            device_id=place(lax.rem(me + d, plane), col + 1),
            device_id_type=MESH,
        )

    @pl.when(has_low)
    def _():
        for d in range(plane):
            send_low(d).start()

    @pl.when(has_high)
    def _():
        for d in range(plane):
            send_high(d).start()

    for d in range(1, plane):
        send_block(d).start()
    own.wait()

    def arrived(dst, sem, z):
        pltpu.make_async_remote_copy(
            src_ref=dst, dst_ref=dst, send_sem=sem, recv_sem=sem,
            device_id=place(me, z), device_id_type=MESH,
        ).wait_recv()

    for m in range(plane):
        t, r = m // rn, m % rn

        @pl.when(me != m)
        def _():
            arrived(gat.at[m], blk_recv.at[m], col)

        for which, (dst, frame) in enumerate(((sx, t + 2), (sg, t))):
            base = frame * pitch + (r * rows + 1) * cols
            v = gat[m, which].astype(jnp.float32)
            dst[1, base : base + cells] = v
            dst[0, base + 1 : base + cells] = v[: cells - 1]
            dst[2, base : base + cells - 1] = v[1:]
            nothing = jnp.zeros((rows, 128), jnp.float32)
            dst[0, pl.ds(base, rows, stride=cols), :] = nothing
            dst[2, pl.ds(base + cols - 1, rows, stride=cols), :] = nothing

    @pl.when(has_low)
    def _():
        for m in range(plane):
            arrived(left.at[m], high_recv.at[m], col - 1)
            for which, (dst, frame) in enumerate(((sx, m // rn + 2), (sg, m // rn))):
                base = frame * pitch + (m % rn * rows + 1) * cols
                dst[0, pl.ds(base, rows, stride=cols), :] = left[m, which].astype(jnp.float32)

    @pl.when(has_high)
    def _():
        for m in range(plane):
            arrived(right.at[m], low_recv.at[m], col + 1)
            for which, (dst, frame) in enumerate(((sx, m // rn + 2), (sg, m // rn))):
                base = frame * pitch + (m % rn * rows + 1) * cols + cols - 1
                dst[2, pl.ds(base, rows, stride=cols), :] = right[m, which].astype(jnp.float32)

    def past(src, base, count):
        for k in range(27):
            a, b, e = k // 9, k // 3 % 3, k % 3
            at = pl.multiple_of(base + a * pitch + b * cols, 8)
            imc[:count, 128 * k : 128 * (k + 1)] = src[e, pl.ds(at, count), :].astype(jnp.bfloat16)

    def future(src, base, count):
        for k in range(27):
            a, b, e = k // 9, k // 3 % 3, k % 3
            at = pl.multiple_of(base + (2 - a) * pitch + (2 - b) * cols, 8)
            imc[:count, 128 * k : 128 * (k + 1)] = src[2 - e, pl.ds(at, count), :].astype(jnp.bfloat16)

    def frame_step(t, carry):
        base = pl.multiple_of(t * pitch, 8)
        past(sx, base, frame_cells)
        hidden = jnp.dot(imc[:frame_cells, :], w1_ref[...], preferred_element_type=jnp.float32)
        future(sg, base, frame_cells)
        grad_act = lax.dot_general(
            imc[:frame_cells, :], w2r[...], NT, preferred_element_type=jnp.float32
        )
        squash = jax.nn.sigmoid(hidden)
        activation = (hidden * squash).astype(jnp.bfloat16)
        grad_hidden = (grad_act * squash * (1.0 + hidden * (1.0 - squash))).astype(jnp.bfloat16)
        at = pl.multiple_of(base + cols, 8)
        sa[pl.ds(pl.multiple_of(at + 2 * pitch, 8), frame_cells), :] = activation.astype(jnp.float32)
        sh[1, pl.ds(at, frame_cells), :] = grad_hidden.astype(jnp.float32)
        return carry

    lax.fori_loop(0, tmn, frame_step, 0)

    lines = tmn * (height + 2)
    edges_out[0] = sh[1, pl.ds(0, lines, stride=cols), :].astype(jnp.bfloat16)
    edges_out[1] = sh[1, pl.ds(cols - 1, lines, stride=cols), :].astype(jnp.bfloat16)

    def send_edge(side):
        return pltpu.make_async_remote_copy(
            src_ref=edges_out.at[side],
            dst_ref=edges_in.at[1 - side],
            send_sem=gh_send.at[side],
            recv_sem=gh_recv.at[1 - side],
            device_id=place(me, col - 1 if side == 0 else col + 1),
            device_id_type=MESH,
        )

    @pl.when(has_low)
    def _():
        send_edge(0).start()

    @pl.when(has_high)
    def _():
        send_edge(1).start()

    picked = jnp.where(
        (lax.broadcasted_iota(jnp.int32, (chunk_pad, 128), 1)
         == me * chunk + lax.broadcasted_iota(jnp.int32, (chunk_pad, 128), 0))
        & (lax.broadcasted_iota(jnp.int32, (chunk_pad, 128), 0) < chunk),
        1.0, 0.0,
    ).astype(jnp.bfloat16)

    def tall(src):
        return lax.dot_general(picked, src.astype(jnp.bfloat16), NT, preferred_element_type=jnp.float32)

    group = slots * chunk_pad // zn

    def packed(tensor):
        for z in range(zn):
            stage[z, tensor] = jnp.concatenate(
                [pp[group * q : group * (q + 1), ochunk * z : ochunk * (z + 1)] for q in range(zn)],
                axis=1,
            ).astype(jnp.bfloat16)

    for e in range(3):
        xt = tall(sx[e])
        for ab in range(9):
            off = ab // 3 * pitch + ab % 3 * cols
            k = 3 * ab + e
            lt[k * chunk_pad : (k + 1) * chunk_pad, :] = xt[:, off : off + span].astype(jnp.bfloat16)
    taps = 27 * chunk_pad
    pp[:taps, :] = jnp.dot(
        lt[:taps, :], sh[1, cols : cols + span, :].astype(jnp.bfloat16),
        preferred_element_type=jnp.float32,
    )
    packed(0)
    at = tall(sa[...])
    for ab in range(9):
        off = ab // 3 * pitch + ab % 3 * cols
        lt[ab * chunk_pad : (ab + 1) * chunk_pad, :] = at[:, off : off + span].astype(jnp.bfloat16)
    for e in range(3):
        part = jnp.dot(
            lt[: 9 * chunk_pad, :], sg[2 - e, cols : cols + span, :].astype(jnp.bfloat16),
            preferred_element_type=jnp.float32,
        )
        for ab in range(9):
            k = 3 * ab + e
            pp[k * chunk_pad : (k + 1) * chunk_pad, :] = part[ab * chunk_pad : (ab + 1) * chunk_pad]
    packed(1)

    def send_piece(z):
        return pltpu.make_async_remote_copy(
            src_ref=stage.at[z],
            dst_ref=landed.at[col],
            send_sem=rs_send.at[z],
            recv_sem=rs_recv.at[col],
            device_id=place(me, z),
            device_id_type=MESH,
        )

    for z in range(zn):

        @pl.when(col != z)
        def _():
            send_piece(z).start()

    sh[0, 1 : span, :] = sh[1, : span - 1, :]
    sh[2, : span - 1, :] = sh[1, 1:span, :]
    nothing = jnp.zeros((lines, 128), jnp.float32)
    sh[0, pl.ds(0, lines, stride=cols), :] = nothing
    sh[2, pl.ds(cols - 1, lines, stride=cols), :] = nothing

    @pl.when(has_low)
    def _():
        arrived(edges_in.at[0], gh_recv.at[0], col - 1)
        sh[0, pl.ds(0, lines, stride=cols), :] = edges_in[0].astype(jnp.float32)

    @pl.when(has_high)
    def _():
        arrived(edges_in.at[1], gh_recv.at[1], col + 1)
        sh[2, pl.ds(cols - 1, lines, stride=cols), :] = edges_in[1].astype(jnp.float32)

    future(sh, pl.multiple_of(tm * pitch + row * cells, 8), cells)
    back_ref[...] = block_ref[1].astype(jnp.float32) + lax.dot_general(
        imc[:cells, :], w1r[...], NT, preferred_element_type=jnp.float32
    )

    acc[...] = stage[col].astype(jnp.float32)
    for z in range(zn):

        @pl.when(col != z)
        def _():
            arrived(landed.at[z], rs_recv.at[z], z)
            acc[...] += landed[z].astype(jnp.float32)

    for tensor, out in enumerate((one_ref, two_ref)):
        got = acc[tensor]
        whole = jnp.concatenate(
            [got[:, ochunk * q : ochunk * (q + 1)] for q in range(zn)], axis=0
        ).reshape(slots, chunk_pad, ochunk)
        out[...] = whole[:27, :chunk, :]

    for d in range(1, plane):
        send_block(d).wait_send()

    @pl.when(has_low)
    def _():
        for d in range(plane):
            send_low(d).wait_send()
        send_edge(0).wait_send()

    @pl.when(has_high)
    def _():
        for d in range(plane):
            send_high(d).wait_send()
        send_edge(1).wait_send()

    for z in range(zn):

        @pl.when(col != z)
        def _():
            send_piece(z).wait_send()


def body(sizes, inputs, cotangent, weight_one, weight_two):
    tmn, rn, zn = sizes
    _, rows, cols, channels = inputs.shape
    plane = tmn * rn
    cells = rows * cols
    chunk = channels // plane
    chunk_pad = max(16, chunk)
    slots = 28
    pitch = (rn * rows + 2) * cols
    total = -(-((tmn + 2) * pitch + 2 * cols) // 128) * 128
    both = jnp.concatenate([inputs, cotangent], axis=0)
    blocks = both.reshape(2, cells, channels)
    edges = jnp.stack([both[:, :, 0], both[:, :, cols - 1]])
    dims = (tmn, rn, zn, rows, cols, chunk, chunk_pad, slots)
    vmem = pl.BlockSpec(memory_space=pltpu.VMEM)
    bf, f32 = jnp.bfloat16, jnp.float32
    group = slots * chunk_pad // zn
    lines = tmn * (rn * rows + 2)
    frame_cells = rn * rows * cols
    dma = pltpu.SemaphoreType.DMA
    back, one, two = pl.pallas_call(
        functools.partial(kernel, dims),
        out_shape=(
            jax.ShapeDtypeStruct((cells, channels), f32),
            jax.ShapeDtypeStruct((27, chunk, channels // zn), f32),
            jax.ShapeDtypeStruct((27, chunk, channels // zn), f32),
        ),
        in_specs=[vmem] * 4,
        out_specs=(vmem,) * 3,
        scratch_shapes=[
            pltpu.VMEM((plane, 2, cells, channels), bf),
            pltpu.VMEM((plane, 2, rows, channels), bf),
            pltpu.VMEM((plane, 2, rows, channels), bf),
            pltpu.VMEM((3, total, channels), f32),
            pltpu.VMEM((3, total, channels), f32),
            pltpu.VMEM((3, total, channels), f32),
            pltpu.VMEM((total, channels), f32),
            pltpu.VMEM((frame_cells, 27 * channels), bf),
            pltpu.VMEM((channels, 27 * channels), bf),
            pltpu.VMEM((channels, 27 * channels), bf),
            pltpu.VMEM((slots * chunk_pad, tmn * pitch), bf),
            pltpu.VMEM((slots * chunk_pad, channels), f32),
            pltpu.VMEM((2, lines, channels), bf),
            pltpu.VMEM((2, lines, channels), bf),
            pltpu.VMEM((zn, 2, group, channels), bf),
            pltpu.VMEM((zn, 2, group, channels), bf),
            pltpu.VMEM((2, group, channels), f32),
            dma,
            dma((plane,)),
            dma((plane,)),
            dma((plane,)),
            dma((plane,)),
            dma((plane,)),
            dma((plane,)),
            dma((2,)),
            dma((2,)),
            dma((zn,)),
            dma((zn,)),
        ],
        compiler_params=pltpu.CompilerParams(
            collective_id=0, has_side_effects=True, vmem_limit_bytes=60 * 1024 * 1024
        ),
    )(blocks, edges, weight_one.reshape(27 * channels, channels), weight_two.reshape(27 * channels, channels))
    return back.reshape(1, rows, cols, channels), one, two


def solution(mesh):
    sizes = (mesh.shape["tm"], mesh.shape["rows"], mesh.shape["cols"])
    placed = (P("tm", "rows", "cols", None), P("tm", "rows", "cols", None), P(), P())
    return jax.shard_map(
        functools.partial(body, sizes),
        mesh=mesh,
        in_specs=placed,
        out_specs=(
            P("tm", "rows", "cols", None),
            P(None, ("tm", "rows"), "cols"),
            P(None, ("tm", "rows"), "cols"),
        ),
        check_vma=False,
    )
```

time: 222 us -> 38 us (0.17)
  waiting for transfers between devices: 136 us -> 0 us
  starting transfers between devices: 46.8 us -> 0 us
  Pallas kernels: 0 us -> 31.1 us
  between operations: 14.6 us -> 0.67 us
  local copies, waits for them, and re-layouts: 18.1 us -> 5.34 us
  matrix products: 5.34 us -> 0 us
    reduce_scatter x4 -> x0, waiting for transfers between devices: 129 us -> none  [the longest x1 42.5 us: body(): lax.psum_scatter(second, ('tm', 'rows'), scatter_dimension=1, tiled=True)]
    ppermute x20 -> x0, starting transfers between devices: 46.6 us -> none  [the longest x8 19.8 us: from_behind(): lax.ppermute(value, axis, [(source, source + steps) for source in range(l...]
    pallas_call x0 -> x1, Pallas kernels: none -> 31.1 us  [body(): pl.pallas_call(functools.partial(kernel, dims), out_shape=(jax.ShapeDtype...]
    reduce_scatter x2 -> x0, local copies, waits for them, and re-layouts: 7.7 us -> none  [the longest x1 3.87 us: body(): lax.psum_scatter(partial_one, 'cols', scatter_dimension=2, tiled=True)]
    ppermute x20 -> x0, waiting for transfers between devices: 6.75 us -> none  [the longest x8 3.85 us: from_behind(): lax.ppermute(value, axis, [(source, source + steps) for source in range(l...]
    dot_general x5 -> x0, matrix products: 5.34 us -> none  [the longest x2 3.43 us: contract_cells(): lax.dot_general(taps, right, (((0,), (0,)), ((), ())), preferred_element_...]
    unnamed x101 -> x8, local copies, waits for them, and re-layouts: 9.52 us -> 4.67 us
  transfers between devices with their start and end apart: 24 -> 0, of which waited for: 9 -> 0; matrix products, arithmetic and copies ran while one was open for 9% -> 0% of each run, Pallas kernels for 0% -> 0%
where the time goes in v1:
time: 38 us; the launch traced here: 37.7 us
  Pallas kernels  31.1 us (82%)
  local copies, waits for them, and re-layouts  5.34 us (14%)
  between operations  0.67 us (2%)
  other arithmetic  0.61 us (2%)
    pallas_call x1, Pallas kernels, body(): pl.pallas_call(functools.partial(kernel, dims), out_shape=(jax.ShapeDtype...  31.1 us
    unnamed x8, local copies, waits for them, and re-layouts  4.67 us

profile of v1, /device:TPU:0, one launch (start us, length us, event | category | flops | bytes accessed | tf_op | source)
XLA Modules:
  0.0 37.7 jit_solution(8827959124310040871)
XLA Ops:
  0.6 0.0 copy-start.1
  0.6 0.8 %copy_dynamic-update-slice_fusion.1 = bf16[2,17,8,128]{3,1,0,2:T(8,128)(2,1)S(1)} fusion(bf16[1,17,8,128]{3,2,1,0:T(8,128)(2,1)} %param.4), kind=kLoop, calls=%fused_computation.2 | loop fusion | bytes 83968
  1.4 0.0 copy-done.1
  1.5 0.7 %copy.15 = bf16[2,17,8,128]{3,2,1,0:T(8,128)(2,1)} copy(bf16[2,17,8,128]{3,1,0,2:T(8,128)(2,1)S(1)} %copy_dynamic-update-slice_fusion) | data formatting | bytes 139264 | tf_op jit(solution)/shard_map/concatenate | solution.py:372
  2.1 0.6 %pad_maximum_fusion.edge_ref = bf16[2,2,17,128]{3,2,1,0:T(8,128)(2,1)} fusion(bf16[1,2,17,128]{3,2,1,0:T(8,128)(2,1)S(1)} %get-tuple-element.10, bf16[1,2,17,128]{3,2,1,0:T(8,128)(2,1)S(1)} %get-tuple-element.9), kind=kLoop, calls=%fused_computation.3 | loop fusion | flops 8704 | bytes 34816 | tf_op jit(solution)/shard_map/stack | solution.py:374
  2.7 31.1 %shard_map.67 = (f32[136,128]{1,0:T(8,128)}, f32[27,16,32]{2,1,0:T(8,128)}, f32[27,16,32]{2,1,0:T(8,128)}) custom-call(bf16[2,136,128]{2,1,0:T(8,128)(2,1)} %bitcast.12, bf16[2,2,17,128]{3,2,1,0:T(8,128)(2,1)} %pad_maximum_fusion.edge_ref, bf16[3456,128]{1,0:T(8,128)(2,1)} %bitcast.10, bf16[3456,128]{1,0:T(8,128)(2,1)} %bitcast.11), custom_call_target="tpu_custom_call" | custom-call | tf_op jit(solution)/shard_map/pallas_call | solution.py:382
  33.8 1.5 %copy.20 = f32[1,17,8,128]{3,2,1,0:T(8,128)} copy(f32[1,17,8,128]{3,2,1,0:T(8,128)} %bitcast.13) | data formatting | bytes 139264
  35.3 0.0 copy-start
  35.3 1.7 %copy.21 = f32[27,16,32]{2,1,0:T(8,128)} copy(f32[27,16,32]{2,1,0:T(8,128)} %get-tuple-element.15) | data formatting | bytes 110592
  37.0 0.0 copy-done
  37.0 0.7 %copy.22 = f32[27,16,32]{2,1,0:T(8,128)} copy(f32[27,16,32]{2,1,0:T(8,128)S(1)} %copy-done) | data formatting | bytes 110592
  (2 shorter events, 0.0 us)
Async XLA Ops:
  0.6 0.8 %copy-start.1 = (bf16[1,17,8,128]{3,2,1,0:T(8,128)(2,1)S(1)}, bf16[1,17,8,128]{3,2,1,0:T(8,128)(2,1)}, u32[]{:S(2)}) copy-start(bf16[1,17,8,128]{3,2,1,0:T(8,128)(2,1)} %param.5) | copy-start | bytes 104452
  35.3 1.7 %copy-start = (f32[27,16,32]{2,1,0:T(8,128)S(1)}, f32[27,16,32]{2,1,0:T(8,128)}, u32[]{:S(2)}) copy-start(f32[27,16,32]{2,1,0:T(8,128)} %get-tuple-element.16) | copy-start | bytes 165892

commit v2 on v1

v2 whole, which is shorter than its diff:
```python
import functools

import jax
import jax.numpy as jnp
from jax import lax
from jax.experimental import pallas as pl
from jax.experimental.pallas import tpu as pltpu
from jax.sharding import PartitionSpec as P

MESH = pl.DeviceIdType.MESH
NT = (((1,), (1,)), ((), ()))


def kernel(
    dims,
    x_ref,
    c_ref,
    w1_ref,
    w2_ref,
    back_ref,
    acc,
    flat,
    edge,
    w1v,
    hid,
    gat,
    left,
    right,
    sx,
    sg,
    sh,
    sa,
    imc,
    w1r,
    w2r,
    lt,
    pp,
    edges_out,
    edges_in,
    stage,
    landed,
    own_sem,
    w1_sem,
    w2_sem,
    blk_send,
    blk_recv,
    low_send,
    low_recv,
    high_send,
    high_recv,
    gh_send,
    gh_recv,
    rs_send,
    rs_recv,
):
    tmn, rn, zn, rows, cols, chunk, chunk_pad, slots = dims
    plane = tmn * rn
    height = rn * rows
    pitch = (height + 2) * cols
    cells = rows * cols
    frame_cells = height * cols
    span = tmn * pitch
    ochunk = 128 // zn
    tm, row, col = lax.axis_index("tm"), lax.axis_index("rows"), lax.axis_index("cols")
    me = tm * rn + row

    def place(index, z):
        return (index // rn, lax.rem(index, rn), z)

    has_low, has_high = col > 0, col < zn - 1

    barrier = pltpu.get_barrier_semaphore()

    def greet(index, z):
        pl.semaphore_signal(barrier, inc=1, device_id=place(index, z), device_id_type=MESH)

    for d in range(1, plane):
        greet(lax.rem(me + d, plane), col)

    @pl.when(has_low)
    def _():
        for d in range(plane):
            greet(lax.rem(me + d, plane), col - 1)

    @pl.when(has_high)
    def _():
        for d in range(plane):
            greet(lax.rem(me + d, plane), col + 1)

    for z in range(zn):

        @pl.when((z > col + 1) | (z < col - 1))
        def _():
            greet(me, z)

    blocks = (x_ref, c_ref)

    def keep(which):
        return pltpu.make_async_copy(blocks[which], gat.at[which, me], own_sem.at[which])

    def load_two(k):
        part = pl.ds(128 * k, 128)
        return pltpu.make_async_copy(w2_ref.at[part, :], w2r.at[:, part], w2_sem.at[k])

    load_one = pltpu.make_async_copy(w1_ref, w1v, w1_sem)
    keep(0).start()
    keep(1).start()
    load_one.start()
    for k in range(27):
        load_two(k).start()

    for which in range(2):
        flat[...] = blocks[which][...].astype(jnp.float32)
        for side in range(2):
            edge[which, side] = flat[pl.ds(side * (cols - 1), rows, stride=cols), :].astype(jnp.bfloat16)
    for buffer in (sx, sg):
        buffer[...] = jnp.zeros(buffer.shape, buffer.dtype)

    beside = jnp.minimum(col, 1) + jnp.minimum(zn - 1 - col, 1)
    pl.semaphore_wait(barrier, plane - 1 + plane * beside + zn - 1 - beside)

    def send_block(which, d):
        peer = lax.rem(me + d, plane)
        return pltpu.make_async_remote_copy(
            src_ref=blocks[which],
            dst_ref=gat.at[which, me],
            send_sem=blk_send.at[which, d],
            recv_sem=blk_recv.at[which, me],
            device_id=place(peer, col),
            device_id_type=MESH,
        )

    def send_low(which, d):
        return pltpu.make_async_remote_copy(
            src_ref=edge.at[which, 0],
            dst_ref=right.at[which, me],
            send_sem=low_send.at[which, d],
            recv_sem=low_recv.at[which, me],
            device_id=place(lax.rem(me + d, plane), col - 1),
            device_id_type=MESH,
        )

    def send_high(which, d):
        return pltpu.make_async_remote_copy(
            src_ref=edge.at[which, 1],
            dst_ref=left.at[which, me],
            send_sem=high_send.at[which, d],
            recv_sem=high_recv.at[which, me],
            device_id=place(lax.rem(me + d, plane), col + 1),
            device_id_type=MESH,
        )

    for which in range(2):
        for d in range(1, plane):
            send_block(which, d).start()

        @pl.when(has_low)
        def _():
            for d in range(plane):
                send_low(which, d).start()

        @pl.when(has_high)
        def _():
            for d in range(plane):
                send_high(which, d).start()

    for buffer in (sh, sa, lt, pp):
        buffer[...] = jnp.zeros(buffer.shape, buffer.dtype)
    load_one.wait()
    for k in range(27):
        w1r[:, 128 * k : 128 * (k + 1)] = w1v[128 * k : 128 * (k + 1), :]
    keep(0).wait()
    keep(1).wait()

    def arrived(dst, sem, z):
        pltpu.make_async_remote_copy(
            src_ref=dst, dst_ref=dst, send_sem=sem, recv_sem=sem,
            device_id=place(me, z), device_id_type=MESH,
        ).wait_recv()

    def gather(which, dst, ahead):
        for m in range(plane):

            @pl.when(me != m)
            def _():
                arrived(gat.at[which, m], blk_recv.at[which, m], col)

            base = (m // rn + ahead) * pitch + (m % rn * rows + 1) * cols
            v = gat[which, m].astype(jnp.float32)
            dst[1, base : base + cells] = v
            dst[0, base + 1 : base + cells] = v[: cells - 1]
            dst[2, base : base + cells - 1] = v[1:]
            nothing = jnp.zeros((rows, 128), jnp.float32)
            dst[0, pl.ds(base, rows, stride=cols), :] = nothing
            dst[2, pl.ds(base + cols - 1, rows, stride=cols), :] = nothing

        @pl.when(has_low)
        def _():
            for m in range(plane):
                arrived(left.at[which, m], high_recv.at[which, m], col - 1)
                base = (m // rn + ahead) * pitch + (m % rn * rows + 1) * cols
                dst[0, pl.ds(base, rows, stride=cols), :] = left[which, m].astype(jnp.float32)

        @pl.when(has_high)
        def _():
            for m in range(plane):
                arrived(right.at[which, m], low_recv.at[which, m], col + 1)
                base = (m // rn + ahead) * pitch + (m % rn * rows + 2) * cols - 1
                dst[2, pl.ds(base, rows, stride=cols), :] = right[which, m].astype(jnp.float32)

    def past(src, base, count):
        for k in range(27):
            a, b, e = k // 9, k // 3 % 3, k % 3
            at = pl.multiple_of(base + a * pitch + b * cols, 8)
            imc[:count, 128 * k : 128 * (k + 1)] = src[e, pl.ds(at, count), :].astype(jnp.bfloat16)

    def future(src, base, count):
        for k in range(27):
            a, b, e = k // 9, k // 3 % 3, k % 3
            at = pl.multiple_of(base + (2 - a) * pitch + (2 - b) * cols, 8)
            imc[:count, 128 * k : 128 * (k + 1)] = src[2 - e, pl.ds(at, count), :].astype(jnp.bfloat16)

    group = slots * chunk_pad // zn
    taps = 27 * chunk_pad
    picked = jnp.where(
        (lax.broadcasted_iota(jnp.int32, (chunk_pad, 128), 1)
         == me * chunk + lax.broadcasted_iota(jnp.int32, (chunk_pad, 128), 0))
        & (lax.broadcasted_iota(jnp.int32, (chunk_pad, 128), 0) < chunk),
        1.0, 0.0,
    ).astype(jnp.bfloat16)

    def tall(src):
        return lax.dot_general(picked, src.astype(jnp.bfloat16), NT, preferred_element_type=jnp.float32)

    def send_piece(tensor, z):
        return pltpu.make_async_remote_copy(
            src_ref=stage.at[tensor, z],
            dst_ref=landed.at[tensor, col],
            send_sem=rs_send.at[tensor, z],
            recv_sem=rs_recv.at[tensor, col],
            device_id=place(me, z),
            device_id_type=MESH,
        )

    def scatter(tensor):
        for z in range(zn):
            stage[tensor, z] = jnp.concatenate(
                [pp[group * q : group * (q + 1), ochunk * z : ochunk * (z + 1)] for q in range(zn)],
                axis=1,
            ).astype(jnp.bfloat16)
        for z in range(zn):

            @pl.when(col != z)
            def _():
                send_piece(tensor, z).start()

    gather(0, sx, 2)

    def forward_step(t, carry):
        base = pl.multiple_of(t * pitch, 8)
        past(sx, base, frame_cells)
        hidden = jnp.dot(imc[:frame_cells, :], w1v[...], preferred_element_type=jnp.float32)
        hid[t] = hidden
        activation = (hidden * jax.nn.sigmoid(hidden)).astype(jnp.bfloat16)
        at = pl.multiple_of(base + cols + 2 * pitch, 8)
        sa[pl.ds(at, frame_cells), :] = activation.astype(jnp.float32)
        return carry

    lax.fori_loop(0, tmn, forward_step, 0)

    gather(1, sg, 0)
    at = tall(sa[...])
    for ab in range(9):
        off = ab // 3 * pitch + ab % 3 * cols
        lt[ab * chunk_pad : (ab + 1) * chunk_pad, :] = at[:, off : off + span].astype(jnp.bfloat16)
    for e in range(3):
        part = jnp.dot(
            lt[: 9 * chunk_pad, :], sg[2 - e, cols : cols + span, :].astype(jnp.bfloat16),
            preferred_element_type=jnp.float32,
        )
        for ab in range(9):
            k = 3 * ab + e
            pp[k * chunk_pad : (k + 1) * chunk_pad, :] = part[ab * chunk_pad : (ab + 1) * chunk_pad]
    scatter(1)

    for k in range(27):
        load_two(k).wait()

    def backward_step(t, carry):
        base = pl.multiple_of(t * pitch, 8)
        future(sg, base, frame_cells)
        grad_act = lax.dot_general(
            imc[:frame_cells, :], w2r[...], NT, preferred_element_type=jnp.float32
        )
        hidden = hid[t]
        squash = jax.nn.sigmoid(hidden)
        grad_hidden = (grad_act * squash * (1.0 + hidden * (1.0 - squash))).astype(jnp.bfloat16)
        at = pl.multiple_of(base + cols, 8)
        sh[1, pl.ds(at, frame_cells), :] = grad_hidden.astype(jnp.float32)
        return carry

    lax.fori_loop(0, tmn, backward_step, 0)

    lines = tmn * (height + 2)
    edges_out[0] = sh[1, pl.ds(0, lines, stride=cols), :].astype(jnp.bfloat16)
    edges_out[1] = sh[1, pl.ds(cols - 1, lines, stride=cols), :].astype(jnp.bfloat16)

    def send_edge(side):
        return pltpu.make_async_remote_copy(
            src_ref=edges_out.at[side],
            dst_ref=edges_in.at[1 - side],
            send_sem=gh_send.at[side],
            recv_sem=gh_recv.at[1 - side],
            device_id=place(me, col - 1 if side == 0 else col + 1),
            device_id_type=MESH,
        )

    @pl.when(has_low)
    def _():
        send_edge(0).start()

    @pl.when(has_high)
    def _():
        send_edge(1).start()

    for e in range(3):
        xt = tall(sx[e])
        for ab in range(9):
            off = ab // 3 * pitch + ab % 3 * cols
            k = 3 * ab + e
            lt[k * chunk_pad : (k + 1) * chunk_pad, :] = xt[:, off : off + span].astype(jnp.bfloat16)
    pp[:taps, :] = jnp.dot(
        lt[:taps, :], sh[1, cols : cols + span, :].astype(jnp.bfloat16),
        preferred_element_type=jnp.float32,
    )
    scatter(0)

    sh[0, 1 : span, :] = sh[1, : span - 1, :]
    sh[2, : span - 1, :] = sh[1, 1:span, :]
    nothing = jnp.zeros((lines, 128), jnp.float32)
    sh[0, pl.ds(0, lines, stride=cols), :] = nothing
    sh[2, pl.ds(cols - 1, lines, stride=cols), :] = nothing

    @pl.when(has_low)
    def _():
        arrived(edges_in.at[0], gh_recv.at[0], col - 1)
        sh[0, pl.ds(0, lines, stride=cols), :] = edges_in[0].astype(jnp.float32)

    @pl.when(has_high)
    def _():
        arrived(edges_in.at[1], gh_recv.at[1], col + 1)
        sh[2, pl.ds(cols - 1, lines, stride=cols), :] = edges_in[1].astype(jnp.float32)

    future(sh, pl.multiple_of(tm * pitch + row * cells, 8), cells)
    back_ref[...] = c_ref[...].astype(jnp.float32) + lax.dot_general(
        imc[:cells, :], w1r[...], NT, preferred_element_type=jnp.float32
    )

    for tensor in (1, 0):
        acc[tensor] = stage[tensor, col].astype(jnp.float32)
        for z in range(zn):

            @pl.when(col != z)
            def _():
                arrived(landed.at[tensor, z], rs_recv.at[tensor, z], z)
                acc[tensor] += landed[tensor, z].astype(jnp.float32)

    for which in range(2):
        for d in range(1, plane):
            send_block(which, d).wait_send()

        @pl.when(has_low)
        def _():
            for d in range(plane):
                send_low(which, d).wait_send()

        @pl.when(has_high)
        def _():
            for d in range(plane):
                send_high(which, d).wait_send()

        for z in range(zn):

            @pl.when(col != z)
            def _():
                send_piece(which, z).wait_send()

    @pl.when(has_low)
    def _():
        send_edge(0).wait_send()

    @pl.when(has_high)
    def _():
        send_edge(1).wait_send()


def finish(zn, chunk, chunk_pad, slots, back_ref, acc_ref, out_ref, one_ref, two_ref):
    ochunk = 128 // zn
    out_ref[...] = back_ref[...]
    for tensor, out in enumerate((one_ref, two_ref)):
        got = acc_ref[tensor]
        whole = jnp.concatenate(
            [got[:, ochunk * q : ochunk * (q + 1)] for q in range(zn)], axis=0
        ).reshape(slots, chunk_pad, ochunk)
        out[...] = whole[:27, :chunk, :]


def body(sizes, inputs, cotangent, weight_one, weight_two):
    tmn, rn, zn = sizes
    _, rows, cols, channels = inputs.shape
    plane = tmn * rn
    cells = rows * cols
    chunk = channels // plane
    chunk_pad = max(16, chunk)
    slots = 28
    pitch = (rn * rows + 2) * cols
    total = -(-((tmn + 2) * pitch + 2 * cols) // 128) * 128
    dims = (tmn, rn, zn, rows, cols, chunk, chunk_pad, slots)
    vmem = pl.BlockSpec(memory_space=pltpu.VMEM)
    bf, f32 = jnp.bfloat16, jnp.float32
    group = slots * chunk_pad // zn
    lines = tmn * (rn * rows + 2)
    frame_cells = rn * rows * cols
    dma = pltpu.SemaphoreType.DMA
    back, acc = pl.pallas_call(
        functools.partial(kernel, dims),
        out_shape=(
            jax.ShapeDtypeStruct((cells, channels), f32),
            jax.ShapeDtypeStruct((2, group, channels), f32),
        ),
        in_specs=[vmem] * 2 + [pl.BlockSpec(memory_space=pl.ANY)] * 2,
        out_specs=(vmem,) * 2,
        scratch_shapes=[
            pltpu.VMEM((cells, channels), f32),
            pltpu.VMEM((2, 2, rows, channels), bf),
            pltpu.VMEM((27 * channels, channels), bf),
            pltpu.VMEM((tmn, frame_cells, channels), f32),
            pltpu.VMEM((2, plane, cells, channels), bf),
            pltpu.VMEM((2, plane, rows, channels), bf),
            pltpu.VMEM((2, plane, rows, channels), bf),
            pltpu.VMEM((3, total, channels), f32),
            pltpu.VMEM((3, total, channels), f32),
            pltpu.VMEM((3, total, channels), f32),
            pltpu.VMEM((total, channels), f32),
            pltpu.VMEM((frame_cells, 27 * channels), bf),
            pltpu.VMEM((channels, 27 * channels), bf),
            pltpu.VMEM((channels, 27 * channels), bf),
            pltpu.VMEM((slots * chunk_pad, tmn * pitch), bf),
            pltpu.VMEM((slots * chunk_pad, channels), f32),
            pltpu.VMEM((2, lines, channels), bf),
            pltpu.VMEM((2, lines, channels), bf),
            pltpu.VMEM((2, zn, group, channels), bf),
            pltpu.VMEM((2, zn, group, channels), bf),
            dma((2,)),
            dma,
            dma((27,)),
            dma((2, plane)),
            dma((2, plane)),
            dma((2, plane)),
            dma((2, plane)),
            dma((2, plane)),
            dma((2, plane)),
            dma((2,)),
            dma((2,)),
            dma((2, zn)),
            dma((2, zn)),
        ],
        compiler_params=pltpu.CompilerParams(
            collective_id=0, has_side_effects=True, vmem_limit_bytes=60 * 1024 * 1024
        ),
    )(
        inputs.reshape(cells, channels),
        cotangent.reshape(cells, channels),
        weight_one.reshape(27 * channels, channels),
        weight_two.reshape(27 * channels, channels),
    )
    back, one, two = pl.pallas_call(
        functools.partial(finish, zn, chunk, chunk_pad, slots),
        out_shape=(
            jax.ShapeDtypeStruct((cells, channels), f32),
            jax.ShapeDtypeStruct((27, chunk, channels // zn), f32),
            jax.ShapeDtypeStruct((27, chunk, channels // zn), f32),
        ),
        in_specs=[vmem] * 2,
        out_specs=(vmem,) * 3,
    )(back, acc)
    return back.reshape(1, rows, cols, channels), one, two


def solution(mesh):
    sizes = (mesh.shape["tm"], mesh.shape["rows"], mesh.shape["cols"])
    placed = (P("tm", "rows", "cols", None), P("tm", "rows", "cols", None), P(), P())
    return jax.shard_map(
        functools.partial(body, sizes),
        mesh=mesh,
        in_specs=placed,
        out_specs=(
            P("tm", "rows", "cols", None),
            P(None, ("tm", "rows"), "cols"),
            P(None, ("tm", "rows"), "cols"),
        ),
        check_vma=False,
    )
```

time: 38 us -> 30.3 us (0.80)
  local copies, waits for them, and re-layouts: 5.34 us -> 0 us
  Pallas kernels: 31.1 us -> 29.5 us
  other arithmetic: 0.61 us -> 0 us
    unnamed x8 -> x0, local copies, waits for them, and re-layouts: 4.67 us -> none
    pallas_call x1, Pallas kernels: 31.1 us -> 27.7 us  [body(): pl.pallas_call(functools.partial(kernel, dims), out_shape=(jax.ShapeDtype...]
    pallas_call x0 -> x1, Pallas kernels: none -> 1.8 us  [body(): pl.pallas_call(functools.partial(finish, zn, chunk, chunk_pad, slots), ou...]
    concatenate x2 -> x0, local copies, waits for them, and re-layouts: 0.67 us -> none  [body(): both = jnp.concatenate([inputs, cotangent], axis=0)]
    another operation x1 -> x0, other arithmetic: 0.61 us -> none  [body(): edges = jnp.stack([both[:, :, 0], both[:, :, cols - 1]])]
where the time goes in v2:
time: 30.3 us; the launch traced here: 30.1 us
  Pallas kernels  29.5 us (97%)
  between operations  0.64 us (2%)
    pallas_call x1, Pallas kernels, body(): pl.pallas_call(functools.partial(kernel, dims), out_shape=(jax.ShapeDtype...  27.7 us
    pallas_call x1, Pallas kernels, body(): pl.pallas_call(functools.partial(finish, zn, chunk, chunk_pad, slots), ou...  1.8 us

profile of v2, /device:TPU:0, one launch (start us, length us, event | category | flops | bytes accessed | tf_op | source)
XLA Modules:
  0.0 30.1 jit_solution(5449059135922754331)
XLA Ops:
  0.6 27.7 %shard_map.67 = (f32[136,128]{1,0:T(8,128)}, f32[2,112,128]{2,1,0:T(8,128)}) custom-call(bf16[136,128]{1,0:T(8,128)(2,1)} %bitcast.7, bf16[136,128]{1,0:T(8,128)(2,1)} %bitcast.8, bf16[3456,128]{1,0:T(8,128)(2,1)} %bitcast.5, bf16[3456,128]{1,0:T(8,128)(2,1)} %bitcast.6), custom_call_target="tpu_custom_call" | custom-call | tf_op jit(solution)/shard_map/pallas_call | solution.py:425
  28.3 1.8 %shard_map.68 = (f32[136,128]{1,0:T(8,128)}, f32[27,16,32]{2,1,0:T(8,128)}, f32[27,16,32]{2,1,0:T(8,128)}) custom-call(f32[136,128]{1,0:T(8,128)} %get-tuple-element.8.back_ref, f32[2,112,128]{2,1,0:T(8,128)} %get-tuple-element.9.acc_ref), custom_call_target="tpu_custom_call" | custom-call | tf_op jit(solution)/shard_map/pallas_call | solution.py:477

commit v3 on v2

--- a/solution.py
+++ b/solution.py
@@ -24,8 +24,7 @@
     w1v,
     hid,
     gat,
-    left,
-    right,
+    hal,
     sx,
     sg,
     sh,
@@ -44,10 +43,10 @@
     w2_sem,
     blk_send,
     blk_recv,
-    low_send,
-    low_recv,
-    high_send,
-    high_recv,
+    edge_send,
+    edge_recv,
+    hal_send,
+    hal_recv,
     gh_send,
     gh_recv,
     rs_send,
@@ -77,21 +76,8 @@
     for d in range(1, plane):
         greet(lax.rem(me + d, plane), col)
 
-    @pl.when(has_low)
-    def _():
-        for d in range(plane):
-            greet(lax.rem(me + d, plane), col - 1)
-
-    @pl.when(has_high)
-    def _():
-        for d in range(plane):
-            greet(lax.rem(me + d, plane), col + 1)
-
-    for z in range(zn):
-
-        @pl.when((z > col + 1) | (z < col - 1))
-        def _():
-            greet(me, z)
+    for step in range(1, zn):
+        greet(me, lax.rem(col + step, zn))
 
     blocks = (x_ref, c_ref)
 
@@ -109,20 +95,38 @@
     for k in range(27):
         load_two(k).start()
 
+    def blank(dst, lead):
+        if lead:
+            dst[:lead, :] = jnp.zeros((lead, 128), jnp.float32)
+        for f in range(tmn):
+            at = lead + f * pitch
+            dst[at : at + cols, :] = jnp.zeros((cols, 128), jnp.float32)
+            dst[at + pitch - cols : at + pitch, :] = jnp.zeros((cols, 128), jnp.float32)
+        at = lead + span
+        dst[at:, :] = jnp.zeros((dst.shape[0] - at, 128), jnp.float32)
+
+    for e in range(3):
+        blank(sx.at[e], 2 * pitch)
     for which in range(2):
-        flat[...] = blocks[which][...].astype(jnp.float32)
+        keep(which).wait()
+        flat[...] = gat[which, me].astype(jnp.float32)
         for side in range(2):
-            edge[which, side] = flat[pl.ds(side * (cols - 1), rows, stride=cols), :].astype(jnp.bfloat16)
-    for buffer in (sx, sg):
-        buffer[...] = jnp.zeros(buffer.shape, buffer.dtype)
-
-    beside = jnp.minimum(col, 1) + jnp.minimum(zn - 1 - col, 1)
-    pl.semaphore_wait(barrier, plane - 1 + plane * beside + zn - 1 - beside)
+            edge[side, which] = flat[pl.ds(side * (cols - 1), rows, stride=cols), :].astype(jnp.bfloat16)
+
+    @pl.when(col == 0)
+    def _():
+        hal[me, 0] = jnp.zeros((2, rows, 128), jnp.bfloat16)
+
+    @pl.when(col == zn - 1)
+    def _():
+        hal[me, 1] = jnp.zeros((2, rows, 128), jnp.bfloat16)
+
+    pl.semaphore_wait(barrier, plane - 1 + zn - 1)
 
     def send_block(which, d):
         peer = lax.rem(me + d, plane)
         return pltpu.make_async_remote_copy(
-            src_ref=blocks[which],
+            src_ref=gat.at[which, me],
             dst_ref=gat.at[which, me],
             send_sem=blk_send.at[which, d],
             recv_sem=blk_recv.at[which, me],
@@ -130,47 +134,44 @@
             device_id_type=MESH,
         )
 
-    def send_low(which, d):
+    def send_rim(side):
         return pltpu.make_async_remote_copy(
-            src_ref=edge.at[which, 0],
-            dst_ref=right.at[which, me],
-            send_sem=low_send.at[which, d],
-            recv_sem=low_recv.at[which, me],
-            device_id=place(lax.rem(me + d, plane), col - 1),
+            src_ref=edge.at[side],
+            dst_ref=hal.at[me, 1 - side],
+            send_sem=edge_send.at[side],
+            recv_sem=edge_recv.at[1 - side],
+            device_id=place(me, col - 1 if side == 0 else col + 1),
             device_id_type=MESH,
         )
 
-    def send_high(which, d):
+    def send_halo(d):
         return pltpu.make_async_remote_copy(
-            src_ref=edge.at[which, 1],
-            dst_ref=left.at[which, me],
-            send_sem=high_send.at[which, d],
-            recv_sem=high_recv.at[which, me],
-            device_id=place(lax.rem(me + d, plane), col + 1),
+            src_ref=hal.at[me],
+            dst_ref=hal.at[me],
+            send_sem=hal_send.at[d],
+            recv_sem=hal_recv.at[me],
+            device_id=place(lax.rem(me + d, plane), col),
             device_id_type=MESH,
         )
 
-    for which in range(2):
-        for d in range(1, plane):
-            send_block(which, d).start()
-
-        @pl.when(has_low)
-        def _():
-            for d in range(plane):
-                send_low(which, d).start()
-
-        @pl.when(has_high)
-        def _():
-            for d in range(plane):
-                send_high(which, d).start()
-
-    for buffer in (sh, sa, lt, pp):
-        buffer[...] = jnp.zeros(buffer.shape, buffer.dtype)
-    load_one.wait()
-    for k in range(27):
-        w1r[:, 128 * k : 128 * (k + 1)] = w1v[128 * k : 128 * (k + 1), :]
-    keep(0).wait()
-    keep(1).wait()
+    @pl.when(has_low)
+    def _():
+        send_rim(0).start()
+
+    @pl.when(has_high)
+    def _():
+        send_rim(1).start()
+
+    for d in range(1, plane):
+        send_block(0, d).start()
+
+    for e in range(3):
+        blank(sg.at[e], 0)
+    blank(sh.at[1], 0)
+    for e in (0, 2):
+        sh[e, span:, :] = jnp.zeros((sh.shape[1] - span, 128), jnp.float32)
+    blank(sa, 2 * pitch)
+    pp[27 * chunk_pad :, :] = jnp.zeros((pp.shape[0] - 27 * chunk_pad, 128), jnp.float32)
 
     def arrived(dst, sem, z):
         pltpu.make_async_remote_copy(
@@ -178,35 +179,39 @@
             device_id=place(me, z), device_id_type=MESH,
         ).wait_recv()
 
+    @pl.when(has_low)
+    def _():
+        arrived(hal.at[me, 0], edge_recv.at[0], col - 1)
+
+    @pl.when(has_high)
+    def _():
+        arrived(hal.at[me, 1], edge_recv.at[1], col + 1)
+
+    for d in range(1, plane):
+        send_halo(d).start()
+    for d in range(1, plane):
+        send_block(1, d).start()
+
+    load_one.wait()
+    for k in range(27):
+        w1r[:, 128 * k : 128 * (k + 1)] = w1v[128 * k : 128 * (k + 1), :]
+
     def gather(which, dst, ahead):
         for m in range(plane):
 
             @pl.when(me != m)
             def _():
                 arrived(gat.at[which, m], blk_recv.at[which, m], col)
+                if which == 0:
+                    arrived(hal.at[m], hal_recv.at[m], col)
 
             base = (m // rn + ahead) * pitch + (m % rn * rows + 1) * cols
             v = gat[which, m].astype(jnp.float32)
             dst[1, base : base + cells] = v
             dst[0, base + 1 : base + cells] = v[: cells - 1]
             dst[2, base : base + cells - 1] = v[1:]
-            nothing = jnp.zeros((rows, 128), jnp.float32)
-            dst[0, pl.ds(base, rows, stride=cols), :] = nothing
-            dst[2, pl.ds(base + cols - 1, rows, stride=cols), :] = nothing
-
-        @pl.when(has_low)
-        def _():
-            for m in range(plane):
-                arrived(left.at[which, m], high_recv.at[which, m], col - 1)
-                base = (m // rn + ahead) * pitch + (m % rn * rows + 1) * cols
-                dst[0, pl.ds(base, rows, stride=cols), :] = left[which, m].astype(jnp.float32)
-
-        @pl.when(has_high)
-        def _():
-            for m in range(plane):
-                arrived(right.at[which, m], low_recv.at[which, m], col + 1)
-                base = (m // rn + ahead) * pitch + (m % rn * rows + 2) * cols - 1
-                dst[2, pl.ds(base, rows, stride=cols), :] = right[which, m].astype(jnp.float32)
+            dst[0, pl.ds(base, rows, stride=cols), :] = hal[m, 0, which].astype(jnp.float32)
+            dst[2, pl.ds(base + cols - 1, rows, stride=cols), :] = hal[m, 1, which].astype(jnp.float32)
 
     def past(src, base, count):
         for k in range(27):
@@ -352,7 +357,7 @@
         sh[2, pl.ds(cols - 1, lines, stride=cols), :] = edges_in[1].astype(jnp.float32)
 
     future(sh, pl.multiple_of(tm * pitch + row * cells, 8), cells)
-    back_ref[...] = c_ref[...].astype(jnp.float32) + lax.dot_general(
+    back_ref[...] = gat[1, me].astype(jnp.float32) + lax.dot_general(
         imc[:cells, :], w1r[...], NT, preferred_element_type=jnp.float32
     )
 
@@ -368,29 +373,23 @@
     for which in range(2):
         for d in range(1, plane):
             send_block(which, d).wait_send()
-
-        @pl.when(has_low)
-        def _():
-            for d in range(plane):
-                send_low(which, d).wait_send()
-
-        @pl.when(has_high)
-        def _():
-            for d in range(plane):
-                send_high(which, d).wait_send()
-
         for z in range(zn):
 
             @pl.when(col != z)
             def _():
                 send_piece(which, z).wait_send()
 
+    for d in range(1, plane):
+        send_halo(d).wait_send()
+
     @pl.when(has_low)
     def _():
+        send_rim(0).wait_send()
         send_edge(0).wait_send()
 
     @pl.when(has_high)
     def _():
+        send_rim(1).wait_send()
         send_edge(1).wait_send()
 
 
@@ -428,7 +427,7 @@
             jax.ShapeDtypeStruct((cells, channels), f32),
             jax.ShapeDtypeStruct((2, group, channels), f32),
         ),
-        in_specs=[vmem] * 2 + [pl.BlockSpec(memory_space=pl.ANY)] * 2,
+        in_specs=[pl.BlockSpec(memory_space=pl.ANY)] * 4,
         out_specs=(vmem,) * 2,
         scratch_shapes=[
             pltpu.VMEM((cells, channels), f32),
@@ -436,8 +435,7 @@
             pltpu.VMEM((27 * channels, channels), bf),
             pltpu.VMEM((tmn, frame_cells, channels), f32),
             pltpu.VMEM((2, plane, cells, channels), bf),
-            pltpu.VMEM((2, plane, rows, channels), bf),
-            pltpu.VMEM((2, plane, rows, channels), bf),
+            pltpu.VMEM((plane, 2, 2, rows, channels), bf),
             pltpu.VMEM((3, total, channels), f32),
             pltpu.VMEM((3, total, channels), f32),
             pltpu.VMEM((3, total, channels), f32),
@@ -456,10 +454,10 @@
             dma((27,)),
             dma((2, plane)),
             dma((2, plane)),
-            dma((2, plane)),
-            dma((2, plane)),
-            dma((2, plane)),
-            dma((2, plane)),
+            dma((2,)),
+            dma((2,)),
+            dma((plane,)),
+            dma((plane,)),
             dma((2,)),
             dma((2,)),
             dma((2, zn)),

time: 30.3 us -> 29.5 us (0.974)
  Pallas kernels: 29.5 us -> 28.7 us
    pallas_call x1, Pallas kernels: 27.7 us -> 26.9 us  [body(): pl.pallas_call(functools.partial(kernel, dims), out_shape=(jax.ShapeDtype...]
where the time goes in v3:
time: 29.5 us; the launch traced here: 29.4 us
  Pallas kernels  28.7 us (97%)
  between operations  0.64 us (2%)
    pallas_call x1, Pallas kernels, body(): pl.pallas_call(functools.partial(kernel, dims), out_shape=(jax.ShapeDtype...  26.9 us
    pallas_call x1, Pallas kernels, body(): pl.pallas_call(functools.partial(finish, zn, chunk, chunk_pad, slots), ou...  1.8 us

profile of v3, /device:TPU:0, one launch (start us, length us, event | category | flops | bytes accessed | tf_op | source)
XLA Modules:
  0.0 29.4 jit_solution(7423977465718805192)
XLA Ops:
  0.6 26.9 %shard_map.67 = (f32[136,128]{1,0:T(8,128)}, f32[2,112,128]{2,1,0:T(8,128)}) custom-call(bf16[136,128]{1,0:T(8,128)(2,1)} %bitcast.7, bf16[136,128]{1,0:T(8,128)(2,1)} %bitcast.8, bf16[3456,128]{1,0:T(8,128)(2,1)} %bitcast.5, bf16[3456,128]{1,0:T(8,128)(2,1)} %bitcast.6), custom_call_target="tpu_custom_call" | custom-call | tf_op jit(solution)/shard_map/pallas_call | solution.py:424
  27.5 1.8 %shard_map.68 = (f32[136,128]{1,0:T(8,128)}, f32[27,16,32]{2,1,0:T(8,128)}, f32[27,16,32]{2,1,0:T(8,128)}) custom-call(f32[136,128]{1,0:T(8,128)} %get-tuple-element.8.back_ref, f32[2,112,128]{2,1,0:T(8,128)} %get-tuple-element.9.acc_ref), custom_call_target="tpu_custom_call" | custom-call | tf_op jit(solution)/shard_map/pallas_call | solution.py:475
